TPU v7x, 32 devices: a whole 2x2x4 slice. The times are simulated.
32 devices in a mesh: dp: 2 (over x), row: 4 (over y, core), col: 4 (over z).
Axes of the slice: x: 2, y: 2, z: 4, core: 2. Of those that a mesh axis runs over, the one named last changes fastest.
Arguments:
- acts: bfloat16 [1024, 8192], P(('dp', 'col'), 'row'), may hold values from -0.5 to 0.5
- grad_out: bfloat16 [1024, 14336], P(('dp', 'row'), 'col'), may hold values from -6 to 6
- weight: bfloat16 [8192, 14336], P('row', 'col'), may hold values from -0.0625 to 0.0625
Outputs:
- grad_input: bfloat16 [1024, 8192], P(('dp', 'col'), 'row')
- grad_weight: bfloat16 [4, 2048, 14336], P('row', 'dp', 'col')
All inputs are finite; a program needn't handle non-finite values.
Results may differ from a plain program's by a relative error of at most 0.001.
Values may be sent and summed in bfloat16 or wider, within the bound.
No kernel may reach another device: no remote copies, remote signals or barrier semaphores. Data moves between devices by JAX's collectives and lax.ppermute only.
A program may use at most 128 MiB of HBM per device.

v0:
```python
import jax
import jax.numpy as jnp
from jax import lax
from jax.sharding import PartitionSpec as P


def shards(acts, grad_out, weight):
    act_local = lax.all_gather(acts, "col", axis=0, tiled=True)
    partial_value = lax.dot_general(
        lax.all_gather(grad_out, "row", axis=0, tiled=True),
        weight,
        (((1,), (1,)), ((), ())),
        preferred_element_type=jnp.float32,
    )
    act_all = lax.all_to_all(act_local, "dp", split_axis=1, concat_axis=0, tiled=True)
    summed = lax.dot_general(
        act_all,
        lax.all_gather(grad_out, ("dp", "row"), axis=0, tiled=True),
        (((0,), (0,)), ((), ())),
        preferred_element_type=jnp.float32,
    )
    grad_weight = summed.astype(jnp.bfloat16)[None]
    grad_input = lax.psum_scatter(partial_value, "col", scatter_dimension=0, tiled=True).astype(
        jnp.bfloat16
    )
    return (grad_input, grad_weight)


def solution(mesh):
    in_specs = (P(("dp", "col"), "row"), P(("dp", "row"), "col"), P("row", "col"))
    out_specs = (P(("dp", "col"), "row"), P("row", "dp", "col"))
    return jax.shard_map(shards, mesh=mesh, in_specs=in_specs, out_specs=out_specs, check_vma=False)
```

profile of v0, /device:TPU:0, one launch (start us, length us, event | category | flops | bytes accessed | tf_op | source)
XLA Modules:
  0.0 239.2 jit_solution(466084870658492629)
XLA Ops:
  7.2 0.0 all-gather.4.cloned.1.call-start
  7.2 0.7 all-gather.4.cloned.1.call-update
  7.9 0.0 all-gather.6.cloned.1.call-start
  7.9 2.0 copy.5
  10.0 0.0 all-gather.6.cloned.1.call-update
  10.0 0.0 all-gather.8.cloned.1.call-start
  10.1 0.7 all-gather.8.cloned.1.call-update
  10.7 0.0 reduce-scatter.2.cloned.1.call-start
  10.8 33.0 %all-gather.4.cloned.1.call-done = bf16[512,3584]{1,0:T(8,128)(2,1)} async-done(((bf16[128,3584]{1,0:T(8,128)(2,1)}), bf16[512,3584]{1,0:T(8,128)(2,1)}) %all-gather.4.cloned.1.call-update) | async-done | bytes 3670032 | tf_op jit(solution)/shard_map/all_gather | solution.py:10
  43.8 13.4 %fusion.1 = f32[512,2048]{1,0:T(8,128)} fusion(bf16[512,3584]{1,0:T(8,128)(2,1)} %all-gather.4.cloned.1.call-done, bf16[2048,3584]{1,0:T(8,128)(2,1)} %param.5), kind=kOutput, calls=%fused_computation.2 | convolution fusion | flops 7516192768 | bytes 22544384 | tf_op jit(solution)/shard_map/dot_general | solution.py:9
  57.2 0.0 reduce-scatter.2.cloned.1.call-update
  57.2 35.0 %all-gather.6.cloned.1.call-done = bf16[512,2048]{0,1:T(8,128)(2,1)} async-done(((bf16[128,2048]{0,1:T(8,128)(2,1)}), bf16[512,2048]{0,1:T(8,128)(2,1)}) %all-gather.6.cloned.1.call-update) | async-done | bytes 2097168 | tf_op jit(solution)/shard_map/all_gather | solution.py:8
  92.2 39.6 %all_to_all.19 = bf16[512,2,1024]{0,2,1:T(8,128)(2,1)S(1)} all-to-all(bf16[512,2,1024]{0,2,1:T(8,128)(2,1)} %bitcast.10), channel_id=1, replica_groups=mesh['dp'=2,'row'=4,'col'=4] {'dp'}, dimensions={1} | all-to-all | bytes 4194304 | tf_op jit(solution)/shard_map/all_to_all | solution.py:15
  131.8 2.5 %copy.6 = bf16[2,512,1024]{2,1,0:T(8,128)(2,1)} copy(bf16[2,512,1024]{1,2,0:T(8,128)(2,1)S(1)} %bitcast.9) | data formatting | bytes 4194304 | tf_op jit(solution)/shard_map/all_to_all | solution.py:15
  134.3 17.7 %all-gather.8.cloned.1.call-done = bf16[1024,3584]{1,0:T(8,128)(2,1)} async-done(((bf16[128,3584]{1,0:T(8,128)(2,1)}), bf16[1024,3584]{1,0:T(8,128)(2,1)}) %all-gather.8.cloned.1.call-update) | async-done | bytes 7340048 | tf_op jit(solution)/shard_map/all_gather | solution.py:18
  151.9 12.6 %fusion = bf16[1,1024,3584]{2,1,0:T(8,128)(2,1)} fusion(bf16[1024,1024]{1,0:T(8,128)(2,1)} %bitcast.11, bf16[1024,3584]{1,0:T(8,128)(2,1)} %all-gather.8.cloned.1.call-done), kind=kOutput, calls=%fused_computation.1 | convolution fusion | flops 7519862784 | bytes 16777216 | tf_op jit(solution)/shard_map/dot_general | solution.py:16
  164.6 66.0 %reduce-scatter.2.cloned.1.call-done = f32[128,2048]{1,0:T(8,128)} async-done(((f32[512,2048]{1,0:T(8,128)}), f32[128,2048]{1,0:T(8,128)}) %reduce-scatter.2.cloned.1.call-update) | async-done | bytes 1048592 | tf_op jit(solution)/shard_map/reduce_scatter | solution.py:23
  230.6 2.1 convert_element_type.6
Async XLA Ops:
  7.2 36.6 %all-gather.4.cloned.1.call-start = ((), (), s32[]{:S(2)}) async-start(), calls=%async_computation.2 | async-start | bytes 4587520 | tf_op jit(solution)/shard_map/all_gather | solution.py:10
  7.9 84.3 %all-gather.6.cloned.1.call-start = ((), (), s32[]{:S(2)}) async-start(), calls=%async_computation.4 | async-start | bytes 2621440 | tf_op jit(solution)/shard_map/all_gather | solution.py:8
  10.0 141.9 %all-gather.8.cloned.1.call-start = ((), (), s32[]{:S(2)}) async-start(), calls=%async_computation.5 | async-start | bytes 8257536 | tf_op jit(solution)/shard_map/all_gather | solution.py:18
  10.7 219.8 %reduce-scatter.2.cloned.1.call-start = ((), (), s32[]{:S(2)}) async-start(), calls=%async_computation.3 | async-start | bytes 5242880 | tf_op jit(solution)/shard_map/reduce_scatter | solution.py:23
Sparse Core Ops, SparseCore 0:
  9.5 34.1 all-gather.3
  45.9 46.2 all-gather.5
  94.1 57.7 all-gather.7
  154.1 76.4 reduce-scatter.1
where the time goes:
time: 239 us
  waiting for transfers between devices  153 us (64%)
  blocking collectives  39.6 us (17%)
  matrix products  26 us (11%)
  between operations  13.8 us (6%)
  local copies, waits for them, and re-layouts  4.51 us (2%)
    reduce_scatter x1, waiting for transfers between devices, shards(): lax.psum_scatter(partial_value, 'col', scatter_dimension=0, tiled=True)  66 us
    all_to_all x1, blocking collectives, shards(): lax.all_to_all(act_local, 'dp', split_axis=1, concat_axis=0, tiled=True)  39.6 us
    all_gather x1, waiting for transfers between devices, shards(): act_local = lax.all_gather(acts, 'col', axis=0, tiled=True)  35 us
    all_gather x1, waiting for transfers between devices, shards(): lax.all_gather(grad_out, 'row', axis=0, tiled=True)  33 us
    all_gather x1, waiting for transfers between devices, shards(): lax.all_gather(grad_out, ('dp', 'row'), axis=0, tiled=True)  17.7 us
    dot_general x1, matrix products, shards(): lax.dot_general(lax.all_gather(grad_out, 'row', axis=0, tiled=True), weig...  13.4 us
    dot_general x1, matrix products, shards(): lax.dot_general(act_all, lax.all_gather(grad_out, ('dp', 'row'), axis=0,...  12.6 us
  transfers between devices with their start and end apart: 4, of which 4 were waited for; matrix products, arithmetic and copies ran while one was open for 13% of the time, Pallas kernels for 0%

commit v1 on v0

--- a/solution.py
+++ b/solution.py
@@ -1,10 +1,208 @@
+import functools
+import math
+
 import jax
 import jax.numpy as jnp
 from jax import lax
+from jax.experimental import pallas as pl
+from jax.experimental.pallas import tpu as pltpu
 from jax.sharding import PartitionSpec as P
 
-
-def shards(acts, grad_out, weight):
+AXES = ("dp", "row", "col")
+
+MU = 16.0
+OFFSET = 124.0
+SLOPE = 2.0 * OFFSET / math.log2(1.0 + MU)
+LANES = 128
+
+
+def encode(z):
+    top = jnp.maximum(jnp.max(jnp.abs(z), axis=1, keepdims=True) * 1.01, 1e-30)
+    top = lax.reduce_precision(top, 8, 7)
+    y = jnp.exp2(SLOPE * jnp.log2(1.0 + jnp.abs(z) * (MU / top)) - OFFSET)
+    y = jnp.where(z < 0, -y, y)
+    top = jnp.broadcast_to(top, (z.shape[0], LANES))
+    return jnp.concatenate([y, top], axis=1).astype(jnp.bfloat16)
+
+
+def decode(code):
+    code = code.astype(jnp.float32)
+    y, top = code[:, :-LANES], code[:, -LANES : 1 - LANES]
+    t = jnp.exp2((jnp.log2(jnp.abs(y)) + OFFSET) * (1.0 / SLOPE)) - 1.0
+    return jnp.where(y < 0, -t, t) * (top * (1.0 / MU))
+
+
+def product(ga, gb, weight):
+    g = jnp.concatenate([ga, gb], axis=0)
+    return lax.dot_general(g, weight, (((1,), (1,)), ((), ())), preferred_element_type=jnp.float32)
+
+
+def grad_kernel(n_blocks, tile, slot_ref, *refs):
+    a_refs, g_refs = refs[:6], refs[6 : 6 + n_blocks]
+    out_ref, a_vmem, at_ref, g_vmem, a_sem, g_sem = refs[6 + n_blocks :]
+    rows = a_refs[0].shape[0]
+    frames = rows // 2
+    t = pl.program_id(0)
+
+    def fetch(step, slot):
+        cols = pl.ds(pl.multiple_of(step * tile, tile), tile)
+        return [
+            pltpu.make_async_copy(
+                ref.at[pl.ds(b * frames, frames), cols],
+                g_vmem.at[slot, pl.ds(i * frames, frames)],
+                g_sem.at[slot, i],
+            )
+            for i, (ref, b) in enumerate(zip(g_refs, BLOCK_OF))
+        ]
+
+    def a_copy(i, k):
+        return pltpu.make_async_copy(a_refs[k], a_vmem.at[i], a_sem.at[i])
+
+    inner = slot_ref[4] != 0
+
+    @pl.when(t == 0)
+    def _():
+        for i in (0, 1):
+            a_copy(i, i).start()
+
+        @pl.when(inner)
+        def _():
+            a_copy(2, 2).start()
+            a_copy(3, 3).start()
+
+        @pl.when(jnp.logical_not(inner))
+        def _():
+            a_copy(2, 4).start()
+            a_copy(3, 5).start()
+
+        for copy in fetch(0, 0):
+            copy.start()
+        for i in range(4):
+            a_copy(i, i).wait()
+            where = pl.ds(pl.multiple_of(slot_ref[i] * rows, rows), rows)
+            at_ref[:, where] = a_vmem[i].T
+
+    slot = lax.rem(t, 2)
+
+    @pl.when(t + 1 < pl.num_programs(0))
+    def _():
+        for copy in fetch(t + 1, 1 - slot):
+            copy.start()
+
+    for copy in fetch(t, slot):
+        copy.wait()
+    full = jnp.dot(at_ref[...], g_vmem[slot], preferred_element_type=jnp.float32)
+    out_ref[...] = full.astype(jnp.bfloat16)[None]
+
+
+BLOCK_OF = (0, 0, 0, 0, 0, 0, 0, 1)
+
+
+def grad(slots, a_blocks, g_parts):
+    rows, width = a_blocks[0].shape
+    depth = g_parts[0][0].shape[1]
+    frames = rows // 2
+    total = frames * len(g_parts)
+    tile = 512
+    return pl.pallas_call(
+        functools.partial(grad_kernel, len(g_parts), tile),
+        grid_spec=pltpu.PrefetchScalarGridSpec(
+            num_scalar_prefetch=1,
+            grid=(depth // tile,),
+            in_specs=[pl.BlockSpec(memory_space=pl.ANY)] * (6 + len(g_parts)),
+            out_specs=pl.BlockSpec((1, width, tile), lambda t, *_: (0, 0, t)),
+            scratch_shapes=[
+                pltpu.VMEM((4, rows, width), jnp.bfloat16),
+                pltpu.VMEM((width, total), jnp.bfloat16),
+                pltpu.VMEM((2, total, tile), jnp.bfloat16),
+                pltpu.SemaphoreType.DMA((4,)),
+                pltpu.SemaphoreType.DMA((2, len(g_parts))),
+            ],
+        ),
+        out_shape=jax.ShapeDtypeStruct((1, width, depth), jnp.bfloat16),
+        cost_estimate=pl.CostEstimate(
+            flops=2 * total * width * depth,
+            bytes_accessed=2 * (width + total) * depth,
+            transcendentals=0,
+        ),
+        name="grad",
+    )(slots, *a_blocks, *[g for g, _ in g_parts])
+
+
+def fast(shape, acts, grad_out, weight):
+    nd, nr, nc = (shape[a] for a in AXES)
+    d, r, c = (lax.axis_index(a) for a in AXES)
+    core = r % 2
+
+    def exchange(x, to):
+        pairs = []
+        for i in range(nd):
+            for j in range(nr):
+                for k in range(nc):
+                    there = to(i, j, k)
+                    if there is not None:
+                        m = (there[0] * nr + there[1]) * nc + there[2]
+                        pairs.append(((i * nr + j) * nc + k, m))
+        return lax.ppermute(x, AXES, pairs)
+
+    over_x = lambda i, j, k: (1 - i, j, k)
+    over_y = lambda i, j, k: (i, j ^ 2, k)
+    over_core = lambda i, j, k: (i, j ^ 1, k)
+    over_z = lambda i, j, k: (i, j, k ^ 1)
+    middle = lambda i, j, k: (i, j, nc - 1 - k) if k in (1, 2) else None
+    outward = lambda i, j, k: (i, j, k ^ 1) if k in (1, 2) else None
+    early_z = lambda i, j, k: (i, j, k ^ 2) if k // 2 != j // 2 else None
+    late_z = lambda i, j, k: (i, j, k ^ 2) if k // 2 == j // 2 else None
+
+    frames, half = grad_out.shape[0], acts.shape[1] // 2
+    scalars = lambda *v: jnp.stack([jnp.asarray(x, jnp.int32) for x in v])
+
+    def pick(z, e):
+        return lax.dynamic_slice_in_dim(z, frames * (e ^ core), frames, 0)
+
+    keep, send = c % 2, 1 - c % 2
+    g1 = exchange(grad_out, over_core)
+    g2 = exchange(grad_out, over_y)
+    other = lax.dynamic_slice_in_dim(acts, (1 - d) * half, half, 1)
+    a_x = exchange(other, over_x)
+    a0 = jnp.concatenate([lax.dynamic_slice_in_dim(acts, d * half, half, 1), a_x], axis=0)
+    a_z = exchange(a0, over_z)
+    a_m = exchange(a0, middle)
+    z_e = product(grad_out, g1, weight)
+    code = encode(pick(z_e, send))
+    e_in = exchange(code, over_z)
+    gx = exchange(grad_out, over_x)
+    g3 = exchange(g2, over_core)
+    a_m2 = exchange(a_z, middle)
+    a_o = exchange(a_m, outward)
+    z_l = product(g2, g3, weight)
+    code = encode(pick(z_l, send))
+    l_in = exchange(code, over_z)
+    e_sum = pick(z_e, keep) + decode(e_in)
+    code = encode(e_sum)
+    e_last = exchange(code, early_z)
+    a_o2 = exchange(a_m2, outward)
+    gxy = exchange(gx, over_y)
+    l_sum = pick(z_l, keep) + decode(l_in)
+    code = encode(l_sum)
+    l_last = exchange(code, late_z)
+    gx2 = jnp.concatenate([gx, gxy], axis=0)
+    gx4 = exchange(gx2, over_core)
+
+    inner = ((c == 1) | (c == 2)).astype(jnp.int32)
+    second = r ^ c ^ (2 + inner)
+    slots = scalars(r ^ c, r ^ c ^ 1, second, second ^ 1, inner)
+    grad_weight = grad(
+        slots,
+        [a0, a_z, a_m, a_m2, a_o, a_o2],
+        [(grad_out, 0), (gx, 0), (g1, 0), (gx4, 0), (g2, 0), (gxy, 0), (g3, 0), (gx4, 1)],
+    )
+    early = r // 2 == c // 2
+    grad_input = jnp.where(early, e_sum, l_sum) + decode(jnp.where(early, e_last, l_last))
+    return grad_input.astype(jnp.bfloat16), grad_weight
+
+
+def general(acts, grad_out, weight):
     act_local = lax.all_gather(acts, "col", axis=0, tiled=True)
     partial_value = lax.dot_general(
         lax.all_gather(grad_out, "row", axis=0, tiled=True),
@@ -29,4 +227,12 @@
 def solution(mesh):
     in_specs = (P(("dp", "col"), "row"), P(("dp", "row"), "col"), P("row", "col"))
     out_specs = (P(("dp", "col"), "row"), P("row", "dp", "col"))
-    return jax.shard_map(shards, mesh=mesh, in_specs=in_specs, out_specs=out_specs, check_vma=False)
+    shape = dict(mesh.shape)
+    specs = dict(mesh=mesh, in_specs=in_specs, out_specs=out_specs, check_vma=False)
+    if (shape["dp"], shape["row"], shape["col"]) != (2, 4, 4):
+        return jax.shard_map(general, **specs)
+
+    def body(*args):
+        return fast(shape, *args)
+
+    return jax.shard_map(body, **specs)

time: 239 us -> 134 us (0.56)
  waiting for transfers between devices: 153 us -> 64.8 us
  blocking collectives: 39.6 us -> 0 us
  starting transfers between devices: 0.16 us -> 22.8 us
  Pallas kernels: 0 us -> 14 us
  between operations: 13.8 us -> 0.82 us
  matrix products: 26 us -> 15.6 us
  other arithmetic: 2.08 us -> 12.3 us
  local copies, waits for them, and re-layouts: 4.51 us -> 1.99 us
    all_gather x3 -> x0, waiting for transfers between devices: 85.7 us -> none  [the longest x1 35 us: shards(): act_local = lax.all_gather(acts, 'col', axis=0, tiled=True)]
    reduce_scatter x1 -> x0, waiting for transfers between devices: 66 us -> none  [shards(): lax.psum_scatter(partial_value, 'col', scatter_dimension=0, tiled=True)]
    ppermute x0 -> x16, waiting for transfers between devices: none -> 64.8 us  [exchange(): return lax.ppermute(x, AXES, pairs)]
    all_to_all x1 -> x0, blocking collectives: 39.6 us -> none  [shards(): lax.all_to_all(act_local, 'dp', split_axis=1, concat_axis=0, tiled=True)]
    ppermute x0 -> x16, starting transfers between devices: none -> 22.8 us  [exchange(): return lax.ppermute(x, AXES, pairs)]
    pallas_call x0 -> x1, Pallas kernels: none -> 14 us  [grad(): pl.pallas_call(functools.partial(grad_kernel, len(g_parts), tile), grid_s...]
    dot_general x2, matrix products: 26 us -> 15.6 us  [product(): lax.dot_general(g, weight, (((1,), (1,)), ((), ())), preferred_element_ty...]
    concatenate x0 -> x6, other arithmetic: none -> 5.57 us  [the longest x1 2.8 us: fast(): gx2 = jnp.concatenate([gx, gxy], axis=0)]
  transfers between devices with their start and end apart: 4 -> 16, of which waited for: 4 -> 6; matrix products, arithmetic and copies ran while one was open for 13% -> 23% of each run, Pallas kernels for 0% -> 0%
where the time goes in v1:
time: 134 us; the launch traced here: 132 us
  waiting for transfers between devices  64.8 us (48%)
  starting transfers between devices  22.8 us (17%)
  matrix products  15.6 us (12%)
  Pallas kernels  14 us (10%)
  other arithmetic  12.3 us (9%)
  local copies, waits for them, and re-layouts  1.99 us (1%)
    ppermute x16, waiting for transfers between devices, exchange(): return lax.ppermute(x, AXES, pairs)  64.8 us
    ppermute x16, starting transfers between devices, exchange(): return lax.ppermute(x, AXES, pairs)  22.8 us
    dot_general x2, matrix products, product(): lax.dot_general(g, weight, (((1,), (1,)), ((), ())), preferred_element_ty...  15.6 us
    pallas_call x1, Pallas kernels, grad(): pl.pallas_call(functools.partial(grad_kernel, len(g_parts), tile), grid_s...  14 us
    concatenate x1, other arithmetic, fast(): gx2 = jnp.concatenate([gx, gxy], axis=0)  2.8 us
  transfers between devices with their start and end apart: 16, of which 6 were waited for; matrix products, arithmetic and copies ran while one was open for 23% of the time, Pallas kernels for 0%

profile of v1, /device:TPU:0, one launch (start us, length us, event | category | flops | bytes accessed | tf_op | source)
XLA Modules:
  0.0 132.4 jit_solution(4695324516070913135)
XLA Ops:
  0.6 0.6 collective-permute-start
  1.2 2.6 %collective-permute-start.13 = (bf16[128,3584]{1,0:T(8,128)(2,1)}, bf16[128,3584]{1,0:T(8,128)(2,1)}, u32[]{:S(2)}, u32[]{:S(2)}) collective-permute-start(bf16[128,3584]{1,0:T(8,128)(2,1)} %refs_6_.1), channel_id=1, source_target_pairs={{0,16},{1,17},{2,18},{3,19},{4,20},{5,21},{6,22},{7,23},{8,24},{9,... | collective-permute-start | bytes 2752520 | tf_op jit(solution)/shard_map/ppermute | solution.py:146
  3.7 1.5 %collective-permute-start.2 = (bf16[128,3584]{1,0:T(8,128)(2,1)}, bf16[128,3584]{1,0:T(8,128)(2,1)}, u32[]{:S(2)}, u32[]{:S(2)}) collective-permute-start(bf16[128,3584]{1,0:T(8,128)(2,1)} %refs_6_.1), channel_id=1, source_target_pairs={{0,8},{1,9},{2,10},{3,11},{4,12},{5,13},{6,14},{7,15},{8,0},{9,1},... | collective-permute-start | bytes 2752520 | tf_op jit(solution)/shard_map/ppermute | solution.py:146
  5.3 1.1 constant_dynamic-slice_fusion.1
  6.3 0.6 collective-permute-start.7
  6.9 7.8 %fusion = f32[256,2048]{1,0:T(8,128)S(1)} fusion(bf16[2048,3584]{1,0:T(8,128)(2,1)} %param.5, bf16[128,3584]{1,0:T(8,128)(2,1)} %collective-permute-done.refs_8_, bf16[128,3584]{1,0:T(8,128)(2,1)} %refs_6_.1), kind=kOutput, calls=%fused_computation | convolution fusion | flops 3761766400 | bytes 18612224 | tf_op jit(solution)/shard_map/dot_general | solution.py:37
  15.6 1.6 %collective-permute-start.1 = (bf16[128,2176]{1,0:T(8,128)(2,1)S(1)}, bf16[128,2176]{1,0:T(8,128)(2,1)}, u32[]{:S(2)}, u32[]{:S(2)}) collective-permute-start(bf16[128,2176]{1,0:T(8,128)(2,1)S(1)} %pad_maximum_fusion.1), channel_id=1, source_target_pairs={{0,1},{1,0},{2,3},{3,2},{4,5},{5,4},{6,7},{7,6},{8,9},{9,8},{10,11... | collective-permute-start | bytes 1671176 | tf_op jit(solution)/shard_map/ppermute | solution.py:146
  17.2 13.4 %collective-permute-done.7 = bf16[128,1024]{1,0:T(8,128)(2,1)} collective-permute-done((bf16[128,1024]{1,0:T(8,128)(2,1)S(1)}, bf16[128,1024]{1,0:T(8,128)(2,1)}, u32[]{:S(2)}, u32[]{:S(2)}) %collective-permute-start.7) | collective-permute-done | bytes 262176 | tf_op jit(solution)/shard_map/ppermute | solution.py:146
  30.6 1.8 %pad_maximum_fusion.5.refs_0_ = bf16[256,1024]{1,0:T(8,128)(2,1)} fusion(bf16[128,1024]{1,0:T(8,128)(2,1)} %collective-permute-done.7, bf16[128,1024]{1,0:T(8,128)(2,1)S(1)} %get-tuple-element.6), kind=kLoop, calls=%fused_computation.36 | loop fusion | flops 1048576 | bytes 1048576 | tf_op jit(solution)/shard_map/concatenate | solution.py:168
  32.4 1.8 %collective-permute-start.8 = (bf16[256,1024]{1,0:T(8,128)(2,1)}, bf16[256,1024]{1,0:T(8,128)(2,1)}, u32[]{:S(2)}, u32[]{:S(2)}) collective-permute-start(bf16[256,1024]{1,0:T(8,128)(2,1)} %pad_maximum_fusion.5.refs_0_), channel_id=1, source_target_pairs={{0,1},{1,0},{2,3},{3,2},{4,5},{5,4},{6,7},{7,6},{8,9},{9,8},{10,11... | collective-permute-start | bytes 1572872 | tf_op jit(solution)/shard_map/ppermute | solution.py:146
  34.2 1.5 %collective-permute-start.9 = (bf16[256,1024]{1,0:T(8,128)(2,1)}, bf16[256,1024]{1,0:T(8,128)(2,1)}, u32[]{:S(2)}, u32[]{:S(2)}) collective-permute-start(bf16[256,1024]{1,0:T(8,128)(2,1)} %pad_maximum_fusion.5.refs_0_), channel_id=1, source_target_pairs={{1,2},{2,1},{5,6},{6,5},{9,10},{10,9},{13,14},{14,13},{17,18},{18,... | collective-permute-start | bytes 1572872 | tf_op jit(solution)/shard_map/ppermute | solution.py:146
  35.7 10.7 %collective-permute-done.8.refs_1_ = bf16[256,1024]{1,0:T(8,128)(2,1)} collective-permute-done((bf16[256,1024]{1,0:T(8,128)(2,1)}, bf16[256,1024]{1,0:T(8,128)(2,1)}, u32[]{:S(2)}, u32[]{:S(2)}) %collective-permute-start.8) | collective-permute-done | bytes 524320 | tf_op jit(solution)/shard_map/ppermute | solution.py:146
  46.4 1.5 %collective-permute-start.10 = (bf16[256,1024]{1,0:T(8,128)(2,1)}, bf16[256,1024]{1,0:T(8,128)(2,1)}, u32[]{:S(2)}, u32[]{:S(2)}) collective-permute-start(bf16[256,1024]{1,0:T(8,128)(2,1)} %collective-permute-done.8.refs_1_), channel_id=1, source_target_pairs={{1,2},{2,1},{5,6},{6,5},{9,10},{10,9},{13,14},{14,13},{17,18},{18,... | collective-permute-start | bytes 1572872 | tf_op jit(solution)/shard_map/ppermute | solution.py:146
  47.9 1.5 %collective-permute-start.14 = (bf16[128,3584]{1,0:T(8,128)(2,1)}, bf16[128,3584]{1,0:T(8,128)(2,1)}, u32[]{:S(2)}, u32[]{:S(2)}) collective-permute-start(bf16[128,3584]{1,0:T(8,128)(2,1)} %collective-permute-done.13.refs_7_), channel_id=1, source_target_pairs={{0,8},{1,9},{2,10},{3,11},{4,12},{5,13},{6,14},{7,15},{8,0},{9,1},... | collective-permute-start | bytes 2752520 | tf_op jit(solution)/shard_map/ppermute | solution.py:146
  49.4 1.1 convert_element_type.19
  50.6 0.6 abs_reduce_fusion.1
  51.3 7.8 %fusion.4 = f32[256,2048]{1,0:T(8,128)S(1)} fusion(bf16[2048,3584]{1,0:T(8,128)(2,1)} %param.5, bf16[128,3584]{1,0:T(8,128)(2,1)} %collective-permute-done.3.refs_12_, bf16[128,3584]{1,0:T(8,128)(2,1)} %collective-permute-done.2.refs_10_), kind=kOutput, calls=%fused_computation.4 | convolution fusion | flops 3761766400 | bytes 18612224 | tf_op jit(solution)/shard_map/dot_general | solution.py:37
  60.0 3.7 %collective-permute-start.4 = (bf16[128,2176]{1,0:T(8,128)(2,1)S(1)}, bf16[128,2176]{1,0:T(8,128)(2,1)S(1)}, u32[]{:S(2)}, u32[]{:S(2)}) collective-permute-start(bf16[128,2176]{1,0:T(8,128)(2,1)S(1)} %pad_maximum_fusion.2), channel_id=1, source_target_pairs={{0,1},{1,0},{2,3},{3,2},{4,5},{5,4},{6,7},{7,6},{8,9},{9,8},{10,11... | collective-permute-start | bytes 1671176 | tf_op jit(solution)/shard_map/ppermute | solution.py:146
  64.4 1.3 collective-permute-start.5
  65.7 17.1 %collective-permute-done.4 = bf16[128,2176]{1,0:T(8,128)(2,1)S(1)} collective-permute-done((bf16[128,2176]{1,0:T(8,128)(2,1)S(1)}, bf16[128,2176]{1,0:T(8,128)(2,1)S(1)}, u32[]{:S(2)}, u32[]{:S(2)}) %collective-permute-start.4) | collective-permute-done | bytes 557088 | tf_op jit(solution)/shard_map/ppermute | solution.py:146
  82.9 0.6 abs_reduce_fusion
  84.2 0.9 pad_maximum_fusion.4
  85.1 2.1 %collective-permute-start.6 = (bf16[128,2176]{1,0:T(8,128)(2,1)}, bf16[128,2176]{1,0:T(8,128)(2,1)}, u32[]{:S(2)}, u32[]{:S(2)}) collective-permute-start(bf16[128,2176]{1,0:T(8,128)(2,1)} %pad_maximum_fusion.4), channel_id=1, source_target_pairs={{0,2},{1,3},{4,6},{5,7},{10,8},{11,9},{14,12},{15,13},{16,18},{17,... | collective-permute-start | bytes 1671176 | tf_op jit(solution)/shard_map/ppermute | solution.py:146
  87.2 2.8 %pad_maximum_fusion = bf16[256,3584]{1,0:T(8,128)(2,1)} fusion(bf16[128,3584]{1,0:T(8,128)(2,1)} %collective-permute-done.14.refs_11_, bf16[128,3584]{1,0:T(8,128)(2,1)} %collective-permute-done.13.refs_7_), kind=kLoop, calls=%fused_computation.8 | loop fusion | flops 3670016 | bytes 3670016 | tf_op jit(solution)/shard_map/concatenate | solution.py:189
  90.0 0.6 stack.23.slot_ref
  90.6 1.3 collective-permute-start.11
  91.9 1.3 collective-permute-start.12
  93.2 3.4 %collective-permute-done.6 = bf16[128,2176]{1,0:T(8,128)(2,1)} collective-permute-done((bf16[128,2176]{1,0:T(8,128)(2,1)}, bf16[128,2176]{1,0:T(8,128)(2,1)}, u32[]{:S(2)}, u32[]{:S(2)}) %collective-permute-start.6) | collective-permute-done | bytes 557088 | tf_op jit(solution)/shard_map/ppermute | solution.py:146
  96.8 1.4 %fusion.18 = bf16[128,2048]{1,0:T(8,128)(2,1)} fusion(f32[128,2048]{1,0:T(8,128)S(1)} %get-tuple-element.5, f32[128,2048]{1,0:T(8,128)S(1)} %get-tuple-element.3, f32[128,2176]{1,0:T(8,128)S(1)} %select_convert_fusion, f32[128]{0:T(128)S(1)} %fusion.19, pred[]{:T(512)S(6)} %eq.13), kind=kLoop, calls=%fused_computation.26 | loop fusion | flops 3145728 | bytes 3670529 | tf_op jit(solution)/shard_map/convert_element_type | solution.py:202
  98.2 9.4 %collective-permute-done.11.refs_4_ = bf16[256,1024]{1,0:T(8,128)(2,1)} collective-permute-done((bf16[256,1024]{1,0:T(8,128)(2,1)}, bf16[256,1024]{1,0:T(8,128)(2,1)}, u32[]{:S(2)}, u32[]{:S(2)}) %collective-permute-start.11) | collective-permute-done | bytes 524320 | tf_op jit(solution)/shard_map/ppermute | solution.py:146
  107.6 10.8 %collective-permute-done.12.refs_5_ = bf16[256,1024]{1,0:T(8,128)(2,1)} collective-permute-done((bf16[256,1024]{1,0:T(8,128)(2,1)}, bf16[256,1024]{1,0:T(8,128)(2,1)}, u32[]{:S(2)}, u32[]{:S(2)}) %collective-permute-start.12) | collective-permute-done | bytes 524320 | tf_op jit(solution)/shard_map/ppermute | solution.py:146
  118.4 14.0 %grad.1 = bf16[1,1024,3584]{2,1,0:T(8,128)(2,1)} custom-call(s32[5]{0:T(128)} %stack.23.slot_ref, bf16[256,1024]{1,0:T(8,128)(2,1)} %pad_maximum_fusion.5.refs_0_, bf16[256,1024]{1,0:T(8,128)(2,1)} %collective-permute-done.8.refs_1_, bf16[256,1024]{1,0:T(8,128)(2,1)} %collective-permute-done.9.refs_2_, bf16[256,1024]{1,0:T(8,128)(2,1)} %collective-permute-done.10.refs_3_, ...), custom_call_target="tpu_custom_call" | custom-call | flops 7516192768 | bytes 14680064 | tf_op jit(solution)/shard_map/grad/pallas_call | solution.py:107
  (34 shorter events, 3.5 us)
Async XLA Ops:
  0.6 6.3 %collective-permute-start = (bf16[128,3584]{1,0:T(8,128)(2,1)}, bf16[128,3584]{1,0:T(8,128)(2,1)}, u32[]{:S(2)}, u32[]{:S(2)}) collective-permute-start(bf16[128,3584]{1,0:T(8,128)(2,1)} %refs_6_.1), channel_id=1, source_target_pairs={{0,4},{1,5},{2,6},{3,7},{4,0},{5,1},{6,2},{7,3},{8,12},{9,13},{10,... | collective-permute-start | bytes 2752520 | tf_op jit(solution)/shard_map/ppermute | solution.py:146
  1.2 46.7 %collective-permute-start.13 = (bf16[128,3584]{1,0:T(8,128)(2,1)}, bf16[128,3584]{1,0:T(8,128)(2,1)}, u32[]{:S(2)}, u32[]{:S(2)}) collective-permute-start(bf16[128,3584]{1,0:T(8,128)(2,1)} %refs_6_.1), channel_id=1, source_target_pairs={{0,16},{1,17},{2,18},{3,19},{4,20},{5,21},{6,22},{7,23},{8,24},{9,... | collective-permute-start | bytes 2752520 | tf_op jit(solution)/shard_map/ppermute | solution.py:146
  3.7 30.5 %collective-permute-start.2 = (bf16[128,3584]{1,0:T(8,128)(2,1)}, bf16[128,3584]{1,0:T(8,128)(2,1)}, u32[]{:S(2)}, u32[]{:S(2)}) collective-permute-start(bf16[128,3584]{1,0:T(8,128)(2,1)} %refs_6_.1), channel_id=1, source_target_pairs={{0,8},{1,9},{2,10},{3,11},{4,12},{5,13},{6,14},{7,15},{8,0},{9,1},... | collective-permute-start | bytes 2752520 | tf_op jit(solution)/shard_map/ppermute | solution.py:146
  6.3 24.3 %collective-permute-start.7 = (bf16[128,1024]{1,0:T(8,128)(2,1)S(1)}, bf16[128,1024]{1,0:T(8,128)(2,1)}, u32[]{:S(2)}, u32[]{:S(2)}) collective-permute-start(bf16[128,1024]{1,0:T(8,128)(2,1)S(1)} %get-tuple-element.7), channel_id=1, source_target_pairs={{0,16},{1,17},{2,18},{3,19},{4,20},{5,21},{6,22},{7,23},{8,24},{9,... | collective-permute-start | bytes 786440 | tf_op jit(solution)/shard_map/ppermute | solution.py:146
  15.6 33.8 %collective-permute-start.1 = (bf16[128,2176]{1,0:T(8,128)(2,1)S(1)}, bf16[128,2176]{1,0:T(8,128)(2,1)}, u32[]{:S(2)}, u32[]{:S(2)}) collective-permute-start(bf16[128,2176]{1,0:T(8,128)(2,1)S(1)} %pad_maximum_fusion.1), channel_id=1, source_target_pairs={{0,1},{1,0},{2,3},{3,2},{4,5},{5,4},{6,7},{7,6},{8,9},{9,8},{10,11... | collective-permute-start | bytes 1671176 | tf_op jit(solution)/shard_map/ppermute | solution.py:146
  32.4 14.0 %collective-permute-start.8 = (bf16[256,1024]{1,0:T(8,128)(2,1)}, bf16[256,1024]{1,0:T(8,128)(2,1)}, u32[]{:S(2)}, u32[]{:S(2)}) collective-permute-start(bf16[256,1024]{1,0:T(8,128)(2,1)} %pad_maximum_fusion.5.refs_0_), channel_id=1, source_target_pairs={{0,1},{1,0},{2,3},{3,2},{4,5},{5,4},{6,7},{7,6},{8,9},{9,8},{10,11... | collective-permute-start | bytes 1572872 | tf_op jit(solution)/shard_map/ppermute | solution.py:146
  34.2 17.0 %collective-permute-start.3 = (bf16[128,3584]{1,0:T(8,128)(2,1)}, bf16[128,3584]{1,0:T(8,128)(2,1)}, u32[]{:S(2)}, u32[]{:S(2)}) collective-permute-start(bf16[128,3584]{1,0:T(8,128)(2,1)} %collective-permute-done.2.refs_10_), channel_id=1, source_target_pairs={{0,4},{1,5},{2,6},{3,7},{4,0},{5,1},{6,2},{7,3},{8,12},{9,13},{10,... | collective-permute-start | bytes 2752520 | tf_op jit(solution)/shard_map/ppermute | solution.py:146
  34.2 56.4 %collective-permute-start.9 = (bf16[256,1024]{1,0:T(8,128)(2,1)}, bf16[256,1024]{1,0:T(8,128)(2,1)}, u32[]{:S(2)}, u32[]{:S(2)}) collective-permute-start(bf16[256,1024]{1,0:T(8,128)(2,1)} %pad_maximum_fusion.5.refs_0_), channel_id=1, source_target_pairs={{1,2},{2,1},{5,6},{6,5},{9,10},{10,9},{13,14},{14,13},{17,18},{18,... | collective-permute-start | bytes 1572872 | tf_op jit(solution)/shard_map/ppermute | solution.py:146
  46.4 45.5 %collective-permute-start.10 = (bf16[256,1024]{1,0:T(8,128)(2,1)}, bf16[256,1024]{1,0:T(8,128)(2,1)}, u32[]{:S(2)}, u32[]{:S(2)}) collective-permute-start(bf16[256,1024]{1,0:T(8,128)(2,1)} %collective-permute-done.8.refs_1_), channel_id=1, source_target_pairs={{1,2},{2,1},{5,6},{6,5},{9,10},{10,9},{13,14},{14,13},{17,18},{18,... | collective-permute-start | bytes 1572872 | tf_op jit(solution)/shard_map/ppermute | solution.py:146
  47.9 39.3 %collective-permute-start.14 = (bf16[128,3584]{1,0:T(8,128)(2,1)}, bf16[128,3584]{1,0:T(8,128)(2,1)}, u32[]{:S(2)}, u32[]{:S(2)}) collective-permute-start(bf16[128,3584]{1,0:T(8,128)(2,1)} %collective-permute-done.13.refs_7_), channel_id=1, source_target_pairs={{0,8},{1,9},{2,10},{3,11},{4,12},{5,13},{6,14},{7,15},{8,0},{9,1},... | collective-permute-start | bytes 2752520 | tf_op jit(solution)/shard_map/ppermute | solution.py:146
  60.0 22.8 %collective-permute-start.4 = (bf16[128,2176]{1,0:T(8,128)(2,1)S(1)}, bf16[128,2176]{1,0:T(8,128)(2,1)S(1)}, u32[]{:S(2)}, u32[]{:S(2)}) collective-permute-start(bf16[128,2176]{1,0:T(8,128)(2,1)S(1)} %pad_maximum_fusion.2), channel_id=1, source_target_pairs={{0,1},{1,0},{2,3},{3,2},{4,5},{5,4},{6,7},{7,6},{8,9},{9,8},{10,11... | collective-permute-start | bytes 1671176 | tf_op jit(solution)/shard_map/ppermute | solution.py:146
  64.4 28.9 %collective-permute-start.5 = (bf16[128,2176]{1,0:T(8,128)(2,1)S(1)}, bf16[128,2176]{1,0:T(8,128)(2,1)S(1)}, u32[]{:S(2)}, u32[]{:S(2)}) collective-permute-start(bf16[128,2176]{1,0:T(8,128)(2,1)S(1)} %pad_maximum_fusion.3), channel_id=1, source_target_pairs={{2,0},{3,1},{6,4},{7,5},{8,10},{9,11},{12,14},{13,15},{18,16},{19,... | collective-permute-start | bytes 1671176 | tf_op jit(solution)/shard_map/ppermute | solution.py:146
  85.1 11.5 %collective-permute-start.6 = (bf16[128,2176]{1,0:T(8,128)(2,1)}, bf16[128,2176]{1,0:T(8,128)(2,1)}, u32[]{:S(2)}, u32[]{:S(2)}) collective-permute-start(bf16[128,2176]{1,0:T(8,128)(2,1)} %pad_maximum_fusion.4), channel_id=1, source_target_pairs={{0,2},{1,3},{4,6},{5,7},{10,8},{11,9},{14,12},{15,13},{16,18},{17,... | collective-permute-start | bytes 1671176 | tf_op jit(solution)/shard_map/ppermute | solution.py:146
  90.0 28.4 %collective-permute-start.15 = (bf16[256,3584]{1,0:T(8,128)(2,1)}, bf16[256,3584]{1,0:T(8,128)(2,1)}, u32[]{:S(2)}, u32[]{:S(2)}) collective-permute-start(bf16[256,3584]{1,0:T(8,128)(2,1)} %pad_maximum_fusion), channel_id=1, source_target_pairs={{0,4},{1,5},{2,6},{3,7},{4,0},{5,1},{6,2},{7,3},{8,12},{9,13},{10,... | collective-permute-start | bytes 5505032 | tf_op jit(solution)/shard_map/ppermute | solution.py:146
  90.6 17.0 %collective-permute-start.11 = (bf16[256,1024]{1,0:T(8,128)(2,1)}, bf16[256,1024]{1,0:T(8,128)(2,1)}, u32[]{:S(2)}, u32[]{:S(2)}) collective-permute-start(bf16[256,1024]{1,0:T(8,128)(2,1)} %collective-permute-done.9.refs_2_), channel_id=1, source_target_pairs={{1,0},{2,3},{5,4},{6,7},{9,8},{10,11},{13,12},{14,15},{17,16},{18,... | collective-permute-start | bytes 1572872 | tf_op jit(solution)/shard_map/ppermute | solution.py:146
  91.9 26.5 %collective-permute-start.12 = (bf16[256,1024]{1,0:T(8,128)(2,1)}, bf16[256,1024]{1,0:T(8,128)(2,1)}, u32[]{:S(2)}, u32[]{:S(2)}) collective-permute-start(bf16[256,1024]{1,0:T(8,128)(2,1)} %collective-permute-done.10.refs_3_), channel_id=1, source_target_pairs={{1,0},{2,3},{5,4},{6,7},{9,8},{10,11},{13,12},{14,15},{17,16},{18,... | collective-permute-start | bytes 1572872 | tf_op jit(solution)/shard_map/ppermute | solution.py:146

commit v2 on v1

--- a/solution.py
+++ b/solution.py
@@ -13,21 +13,21 @@
 MU = 16.0
 OFFSET = 124.0
 SLOPE = 2.0 * OFFSET / math.log2(1.0 + MU)
-LANES = 128
+SCALE_ROWS = 8
 
 
 def encode(z):
-    top = jnp.maximum(jnp.max(jnp.abs(z), axis=1, keepdims=True) * 1.01, 1e-30)
+    top = jnp.maximum(jnp.max(jnp.abs(z), axis=0, keepdims=True) * 1.01, 1e-30)
     top = lax.reduce_precision(top, 8, 7)
     y = jnp.exp2(SLOPE * jnp.log2(1.0 + jnp.abs(z) * (MU / top)) - OFFSET)
-    y = jnp.where(z < 0, -y, y)
-    top = jnp.broadcast_to(top, (z.shape[0], LANES))
-    return jnp.concatenate([y, top], axis=1).astype(jnp.bfloat16)
+    y = jnp.where(z < 0, -y, y).astype(jnp.bfloat16)
+    top = jnp.broadcast_to(top.astype(jnp.bfloat16), (SCALE_ROWS, z.shape[1]))
+    return jnp.concatenate([y, top], axis=0)
 
 
 def decode(code):
-    code = code.astype(jnp.float32)
-    y, top = code[:, :-LANES], code[:, -LANES : 1 - LANES]
+    y = code[:-SCALE_ROWS].astype(jnp.float32)
+    top = code[-SCALE_ROWS : 1 - SCALE_ROWS].astype(jnp.float32)
     t = jnp.exp2((jnp.log2(jnp.abs(y)) + OFFSET) * (1.0 / SLOPE)) - 1.0
     return jnp.where(y < 0, -t, t) * (top * (1.0 / MU))
 
@@ -48,11 +48,11 @@
         cols = pl.ds(pl.multiple_of(step * tile, tile), tile)
         return [
             pltpu.make_async_copy(
-                ref.at[pl.ds(b * frames, frames), cols],
+                ref.at[:, cols],
                 g_vmem.at[slot, pl.ds(i * frames, frames)],
                 g_sem.at[slot, i],
             )
-            for i, (ref, b) in enumerate(zip(g_refs, BLOCK_OF))
+            for i, ref in enumerate(g_refs)
         ]
 
     def a_copy(i, k):
@@ -95,12 +95,9 @@
     out_ref[...] = full.astype(jnp.bfloat16)[None]
 
 
-BLOCK_OF = (0, 0, 0, 0, 0, 0, 0, 1)
-
-
 def grad(slots, a_blocks, g_parts):
     rows, width = a_blocks[0].shape
-    depth = g_parts[0][0].shape[1]
+    depth = g_parts[0].shape[1]
     frames = rows // 2
     total = frames * len(g_parts)
     tile = 512
@@ -126,7 +123,7 @@
             transcendentals=0,
         ),
         name="grad",
-    )(slots, *a_blocks, *[g for g, _ in g_parts])
+    )(slots, *a_blocks, *g_parts)
 
 
 def fast(shape, acts, grad_out, weight):
@@ -151,7 +148,20 @@
     over_z = lambda i, j, k: (i, j, k ^ 1)
     middle = lambda i, j, k: (i, j, nc - 1 - k) if k in (1, 2) else None
     outward = lambda i, j, k: (i, j, k ^ 1) if k in (1, 2) else None
-    early_z = lambda i, j, k: (i, j, k ^ 2) if k // 2 != j // 2 else None
+
+
+    def line(j, k):
+        return k if j // 2 else nc - 1 - k
+
+    def along(*moves):
+        to = dict(moves)
+
+        def there(i, j, k):
+            q = to.get(line(j, k))
+            return None if q is None else (i, j, q if j // 2 else nc - 1 - q)
+
+        return there
+
     late_z = lambda i, j, k: (i, j, k ^ 2) if k // 2 == j // 2 else None
 
     frames, half = grad_out.shape[0], acts.shape[1] // 2
@@ -169,8 +179,10 @@
     a_z = exchange(a0, over_z)
     a_m = exchange(a0, middle)
     z_e = product(grad_out, g1, weight)
-    code = encode(pick(z_e, send))
-    e_in = exchange(code, over_z)
+    q = jnp.where(r // 2 == 1, c, nc - 1 - c)
+    far, near = r // 2, 1 - r // 2
+    code = encode(pick(z_e, jnp.where(q == 0, far, near)))
+    e_one = exchange(code, along((0, 1), (3, 2)))
     gx = exchange(grad_out, over_x)
     g3 = exchange(g2, over_core)
     a_m2 = exchange(a_z, middle)
@@ -178,16 +190,21 @@
     z_l = product(g2, g3, weight)
     code = encode(pick(z_l, send))
     l_in = exchange(code, over_z)
-    e_sum = pick(z_e, keep) + decode(e_in)
-    code = encode(e_sum)
-    e_last = exchange(code, early_z)
+    e_part = decode(e_one)
+    code = encode(pick(z_e, jnp.where(q == 0, near, far)) + e_part)
+    e_sum = lax.optimization_barrier(pick(z_e, jnp.where(q == 3, far, near)) + e_part)
+    e_two = exchange(code, along((0, 1), (1, 2)))
     a_o2 = exchange(a_m2, outward)
     gxy = exchange(gx, over_y)
+    gx1 = exchange(gx, over_core)
     l_sum = pick(z_l, keep) + decode(l_in)
     code = encode(l_sum)
+    l_sum = lax.optimization_barrier(l_sum)
     l_last = exchange(code, late_z)
-    gx2 = jnp.concatenate([gx, gxy], axis=0)
-    gx4 = exchange(gx2, over_core)
+    base = lax.optimization_barrier(jnp.where(r // 2 == c // 2, e_sum, l_sum))
+    code = encode(pick(z_e, jnp.where(q == 1, near, far)) + decode(e_two))
+    e_three = exchange(code, along((1, 2), (2, 3)))
+    gx3 = exchange(gxy, over_core)
 
     inner = ((c == 1) | (c == 2)).astype(jnp.int32)
     second = r ^ c ^ (2 + inner)
@@ -195,10 +212,9 @@
     grad_weight = grad(
         slots,
         [a0, a_z, a_m, a_m2, a_o, a_o2],
-        [(grad_out, 0), (gx, 0), (g1, 0), (gx4, 0), (g2, 0), (gxy, 0), (g3, 0), (gx4, 1)],
-    )
-    early = r // 2 == c // 2
-    grad_input = jnp.where(early, e_sum, l_sum) + decode(jnp.where(early, e_last, l_last))
+        [grad_out, gx, g1, gx1, g2, gxy, g3, gx3],
+    )
+    grad_input = base + decode(e_three.astype(jnp.float32) + l_last.astype(jnp.float32))
     return grad_input.astype(jnp.bfloat16), grad_weight
 
 

time: 134 us -> 114 us (0.85)
  the two profiles are of different devices: /device:TPU:0 before, /device:TPU:4 now
where the time goes in v2:
time: 114 us; the launch traced here: 113 us
  waiting for transfers between devices  39.6 us (35%)
  starting transfers between devices  33.4 us (29%)
  matrix products  15.4 us (14%)
  Pallas kernels  14 us (12%)
  other arithmetic  7.98 us (7%)
  local copies, waits for them, and re-layouts  1.79 us (2%)
    ppermute x18, waiting for transfers between devices, exchange(): return lax.ppermute(x, AXES, pairs)  39.6 us
    ppermute x18, starting transfers between devices, exchange(): return lax.ppermute(x, AXES, pairs)  33.4 us
    dot_general x2, matrix products, product(): lax.dot_general(g, weight, (((1,), (1,)), ((), ())), preferred_element_ty...  15.4 us
    pallas_call x1, Pallas kernels, grad(): pl.pallas_call(functools.partial(grad_kernel, len(g_parts), tile), grid_s...  14 us
    convert_element_type x5, other arithmetic, encode(): y = jnp.where(z < 0, -y, y).astype(jnp.bfloat16)  3.43 us
  transfers between devices with their start and end apart: 18, of which 6 were waited for; matrix products, arithmetic and copies ran while one was open for 21% of the time, Pallas kernels for 12%

profile of v2, /device:TPU:4, one launch (start us, length us, event | category | flops | bytes accessed | tf_op | source)
XLA Modules:
  0.0 113.1 jit_solution(4478935887507591157)
XLA Ops:
  0.7 1.1 constant_dynamic-slice_fusion.1
  1.9 1.6 %collective-permute-start.8 = (bf16[128,1024]{1,0:T(8,128)(2,1)S(1)}, bf16[128,1024]{1,0:T(8,128)(2,1)S(1)}, u32[]{:S(2)}, u32[]{:S(2)}) collective-permute-start(bf16[128,1024]{1,0:T(8,128)(2,1)S(1)} %get-tuple-element.7), channel_id=1, source_target_pairs={{0,16},{1,17},{2,18},{3,19},{4,20},{5,21},{6,22},{7,23},{8,24},{9,... | collective-permute-start | bytes 786440 | tf_op jit(solution)/shard_map/ppermute | solution.py:143
  3.4 0.5 collective-permute-start.14
  4.0 7.1 %collective-permute-done.8 = bf16[128,1024]{1,0:T(8,128)(2,1)S(1)} collective-permute-done((bf16[128,1024]{1,0:T(8,128)(2,1)S(1)}, bf16[128,1024]{1,0:T(8,128)(2,1)S(1)}, u32[]{:S(2)}, u32[]{:S(2)}) %collective-permute-start.8) | collective-permute-done | bytes 262176 | tf_op jit(solution)/shard_map/ppermute | solution.py:143
  11.1 0.8 pad_maximum_fusion.5.refs_0_
  11.9 1.6 %collective-permute-start.9 = (bf16[256,1024]{1,0:T(8,128)(2,1)}, bf16[256,1024]{1,0:T(8,128)(2,1)}, u32[]{:S(2)}, u32[]{:S(2)}) collective-permute-start(bf16[256,1024]{1,0:T(8,128)(2,1)} %pad_maximum_fusion.5.refs_0_), channel_id=1, source_target_pairs={{0,1},{1,0},{2,3},{3,2},{4,5},{5,4},{6,7},{7,6},{8,9},{9,8},{10,11... | collective-permute-start | bytes 1572872 | tf_op jit(solution)/shard_map/ppermute | solution.py:143
  13.5 7.5 %fusion = f32[256,2048]{1,0:T(8,128)S(1)} fusion(bf16[2048,3584]{1,0:T(8,128)(2,1)} %param.5, bf16[128,3584]{1,0:T(8,128)(2,1)} %collective-permute-done.refs_8_, bf16[128,3584]{1,0:T(8,128)(2,1)S(1)} %copy-done), kind=kOutput, calls=%fused_computation | convolution fusion | flops 3761766400 | bytes 18612224 | tf_op jit(solution)/shard_map/dot_general | solution.py:37
  21.7 2.4 %collective-permute-start.1 = (bf16[136,2048]{1,0:T(8,128)(2,1)S(1)}, bf16[136,2048]{1,0:T(8,128)(2,1)S(1)}, u32[]{:S(2)}, u32[]{:S(2)}) collective-permute-start(bf16[136,2048]{1,0:T(8,128)(2,1)S(1)} %pad_maximum_fusion), channel_id=1, source_target_pairs={{0,1},{3,2},{4,5},{7,6},{8,9},{11,10},{12,13},{15,14},{16,17},{19,... | collective-permute-start | bytes 1671176 | tf_op jit(solution)/shard_map/ppermute | solution.py:143
  24.1 1.5 %collective-permute-start.10 = (bf16[256,1024]{1,0:T(8,128)(2,1)}, bf16[256,1024]{1,0:T(8,128)(2,1)}, u32[]{:S(2)}, u32[]{:S(2)}) collective-permute-start(bf16[256,1024]{1,0:T(8,128)(2,1)} %pad_maximum_fusion.5.refs_0_), channel_id=1, source_target_pairs={{1,2},{2,1},{5,6},{6,5},{9,10},{10,9},{13,14},{14,13},{17,18},{18,... | collective-permute-start | bytes 1572872 | tf_op jit(solution)/shard_map/ppermute | solution.py:143
  25.6 1.5 %collective-permute-start.11 = (bf16[256,1024]{1,0:T(8,128)(2,1)}, bf16[256,1024]{1,0:T(8,128)(2,1)}, u32[]{:S(2)}, u32[]{:S(2)}) collective-permute-start(bf16[256,1024]{1,0:T(8,128)(2,1)} %collective-permute-done.9.refs_1_), channel_id=1, source_target_pairs={{1,2},{2,1},{5,6},{6,5},{9,10},{10,9},{13,14},{14,13},{17,18},{18,... | collective-permute-start | bytes 1572872 | tf_op jit(solution)/shard_map/ppermute | solution.py:143
  27.1 0.6 stack.23.slot_ref
  27.7 1.3 %collective-permute-start.12 = (bf16[256,1024]{1,0:T(8,128)(2,1)}, bf16[256,1024]{1,0:T(8,128)(2,1)}, u32[]{:S(2)}, u32[]{:S(2)}) collective-permute-start(bf16[256,1024]{1,0:T(8,128)(2,1)} %collective-permute-done.10.refs_2_), channel_id=1, source_target_pairs={{1,0},{2,3},{5,4},{6,7},{9,8},{10,11},{13,12},{14,15},{17,16},{18,... | collective-permute-start | bytes 1572872 | tf_op jit(solution)/shard_map/ppermute | solution.py:143
  29.0 1.4 %collective-permute-done.14.refs_7_ = bf16[128,3584]{1,0:T(8,128)(2,1)} collective-permute-done((bf16[128,3584]{1,0:T(8,128)(2,1)}, bf16[128,3584]{1,0:T(8,128)(2,1)}, u32[]{:S(2)}, u32[]{:S(2)}) %collective-permute-start.14) | collective-permute-done | bytes 917536 | tf_op jit(solution)/shard_map/ppermute | solution.py:143
  30.6 0.5 collective-permute-start.3
  31.1 5.0 %collective-permute-done.1 = bf16[136,2048]{1,0:T(8,128)(2,1)S(1)} collective-permute-done((bf16[136,2048]{1,0:T(8,128)(2,1)S(1)}, bf16[136,2048]{1,0:T(8,128)(2,1)S(1)}, u32[]{:S(2)}, u32[]{:S(2)}) %collective-permute-start.1) | collective-permute-done | bytes 557088 | tf_op jit(solution)/shard_map/ppermute | solution.py:143
  36.1 1.3 %collective-permute-start.13 = (bf16[256,1024]{1,0:T(8,128)(2,1)}, bf16[256,1024]{1,0:T(8,128)(2,1)}, u32[]{:S(2)}, u32[]{:S(2)}) collective-permute-start(bf16[256,1024]{1,0:T(8,128)(2,1)} %collective-permute-done.11.refs_3_), channel_id=1, source_target_pairs={{1,0},{2,3},{5,4},{6,7},{9,8},{10,11},{13,12},{14,15},{17,16},{18,... | collective-permute-start | bytes 1572872 | tf_op jit(solution)/shard_map/ppermute | solution.py:143
  37.4 0.6 abs_reduce_fusion.2
  38.0 1.0 fusion.31
  39.1 17.2 %collective-permute-start.5 = (bf16[136,2048]{1,0:T(8,128)(2,1)S(1)}, bf16[136,2048]{1,0:T(8,128)(2,1)S(1)}, u32[]{:S(2)}, u32[]{:S(2)}) collective-permute-start(bf16[136,2048]{1,0:T(8,128)(2,1)S(1)} %pad_maximum_fusion.2), channel_id=1, source_target_pairs={{2,1},{3,2},{6,5},{7,6},{8,9},{9,10},{12,13},{13,14},{18,17},{19,1... | collective-permute-start | bytes 1671176 | tf_op jit(solution)/shard_map/ppermute | solution.py:143
  56.3 7.8 %fusion.4 = f32[256,2048]{1,0:T(8,128)S(1)} fusion(bf16[2048,3584]{1,0:T(8,128)(2,1)} %param.5, bf16[128,3584]{1,0:T(8,128)(2,1)} %collective-permute-done.3.refs_12_, bf16[128,3584]{1,0:T(8,128)(2,1)} %collective-permute-done.2.refs_10_), kind=kOutput, calls=%fused_computation.4 | convolution fusion | flops 3761766400 | bytes 18612224 | tf_op jit(solution)/shard_map/dot_general | solution.py:37
  64.8 1.8 %collective-permute-start.4 = (bf16[136,2048]{1,0:T(8,128)(2,1)S(1)}, bf16[136,2048]{1,0:T(8,128)(2,1)S(1)}, u32[]{:S(2)}, u32[]{:S(2)}) collective-permute-start(bf16[136,2048]{1,0:T(8,128)(2,1)S(1)} %pad_maximum_fusion.1), channel_id=1, source_target_pairs={{0,1},{1,0},{2,3},{3,2},{4,5},{5,4},{6,7},{7,6},{8,9},{9,8},{10,11... | collective-permute-start | bytes 1671176 | tf_op jit(solution)/shard_map/ppermute | solution.py:143
  66.6 2.7 %collective-permute-done.5 = bf16[136,2048]{1,0:T(8,128)(2,1)S(1)} collective-permute-done((bf16[136,2048]{1,0:T(8,128)(2,1)S(1)}, bf16[136,2048]{1,0:T(8,128)(2,1)S(1)}, u32[]{:S(2)}, u32[]{:S(2)}) %collective-permute-start.5) | collective-permute-done | bytes 557088 | tf_op jit(solution)/shard_map/ppermute | solution.py:143
  69.3 0.6 abs_reduce_fusion.1
  69.9 1.0 fusion.34
  71.0 9.8 %collective-permute-done.4 = bf16[136,2048]{1,0:T(8,128)(2,1)S(1)} collective-permute-done((bf16[136,2048]{1,0:T(8,128)(2,1)S(1)}, bf16[136,2048]{1,0:T(8,128)(2,1)S(1)}, u32[]{:S(2)}, u32[]{:S(2)}) %collective-permute-start.4) | collective-permute-done | bytes 557088 | tf_op jit(solution)/shard_map/ppermute | solution.py:143
  80.8 0.7 collective-permute-start.6
  81.5 0.6 abs_reduce_fusion
  82.2 0.5 fusion.35
  82.8 1.3 %collective-permute-start.7 = (bf16[136,2048]{1,0:T(8,128)(2,1)S(1)}, bf16[136,2048]{1,0:T(8,128)(2,1)S(1)}, u32[]{:S(2)}, u32[]{:S(2)}) collective-permute-start(bf16[136,2048]{1,0:T(8,128)(2,1)S(1)} %pad_maximum_fusion.4), channel_id=1, source_target_pairs={{0,2},{1,3},{4,6},{5,7},{10,8},{11,9},{14,12},{15,13},{16,18},{17,... | collective-permute-start | bytes 1671176 | tf_op jit(solution)/shard_map/ppermute | solution.py:143
  84.1 14.0 %grad.1 = bf16[1,1024,3584]{2,1,0:T(8,128)(2,1)} custom-call(s32[5]{0:T(128)} %stack.23.slot_ref, bf16[256,1024]{1,0:T(8,128)(2,1)} %pad_maximum_fusion.5.refs_0_, bf16[256,1024]{1,0:T(8,128)(2,1)} %collective-permute-done.9.refs_1_, bf16[256,1024]{1,0:T(8,128)(2,1)} %collective-permute-done.10.refs_2_, bf16[256,1024]{1,0:T(8,128)(2,1)} %collective-permute-done.11.refs_3_, ...), custom_call_target="tpu_custom_call" | custom-call | flops 7516192768 | bytes 14680064 | tf_op jit(solution)/shard_map/grad/pallas_call | solution.py:104
  98.1 13.6 %collective-permute-done.7 = bf16[136,2048]{1,0:T(8,128)(2,1)S(1)} collective-permute-done((bf16[136,2048]{1,0:T(8,128)(2,1)S(1)}, bf16[136,2048]{1,0:T(8,128)(2,1)S(1)}, u32[]{:S(2)}, u32[]{:S(2)}) %collective-permute-start.7) | collective-permute-done | bytes 557088 | tf_op jit(solution)/shard_map/ppermute | solution.py:143
  111.8 1.3 %fusion.38 = bf16[128,2048]{1,0:T(8,128)(2,1)} fusion(f32[128,2048]{1,0:T(8,128)S(1)} %broadcast_select_fusion, f32[136,2048]{1,0:T(8,128)S(1)} %convert_add_fusion, f32[2048]{0:T(1024)S(1)} %bitcast.16), kind=kLoop, calls=%fused_computation.54 | loop fusion | flops 2883584 | bytes 2629632 | tf_op jit(solution)/shard_map/convert_element_type | solution.py:218
  (44 shorter events, 2.1 us)
Async XLA Ops:
  0.6 12.9 %copy-start = (bf16[128,3584]{1,0:T(8,128)(2,1)S(1)}, bf16[128,3584]{1,0:T(8,128)(2,1)}, u32[]{:S(2)}) copy-start(bf16[128,3584]{1,0:T(8,128)(2,1)} %refs_6_.1) | copy-start | bytes 2752516
  0.6 12.9 %collective-permute-start = (bf16[128,3584]{1,0:T(8,128)(2,1)}, bf16[128,3584]{1,0:T(8,128)(2,1)}, u32[]{:S(2)}, u32[]{:S(2)}) collective-permute-start(bf16[128,3584]{1,0:T(8,128)(2,1)} %refs_6_.1), channel_id=1, source_target_pairs={{0,4},{1,5},{2,6},{3,7},{4,0},{5,1},{6,2},{7,3},{8,12},{9,13},{10,... | collective-permute-start | bytes 2752520 | tf_op jit(solution)/shard_map/ppermute | solution.py:143
  1.9 9.2 %collective-permute-start.8 = (bf16[128,1024]{1,0:T(8,128)(2,1)S(1)}, bf16[128,1024]{1,0:T(8,128)(2,1)S(1)}, u32[]{:S(2)}, u32[]{:S(2)}) collective-permute-start(bf16[128,1024]{1,0:T(8,128)(2,1)S(1)} %get-tuple-element.7), channel_id=1, source_target_pairs={{0,16},{1,17},{2,18},{3,19},{4,20},{5,21},{6,22},{7,23},{8,24},{9,... | collective-permute-start | bytes 786440 | tf_op jit(solution)/shard_map/ppermute | solution.py:143
  3.4 26.9 %collective-permute-start.14 = (bf16[128,3584]{1,0:T(8,128)(2,1)}, bf16[128,3584]{1,0:T(8,128)(2,1)}, u32[]{:S(2)}, u32[]{:S(2)}) collective-permute-start(bf16[128,3584]{1,0:T(8,128)(2,1)} %refs_6_.1), channel_id=1, source_target_pairs={{0,16},{1,17},{2,18},{3,19},{4,20},{5,21},{6,22},{7,23},{8,24},{9,... | collective-permute-start | bytes 2752520 | tf_op jit(solution)/shard_map/ppermute | solution.py:143
  4.0 26.6 %collective-permute-start.2 = (bf16[128,3584]{1,0:T(8,128)(2,1)}, bf16[128,3584]{1,0:T(8,128)(2,1)}, u32[]{:S(2)}, u32[]{:S(2)}) collective-permute-start(bf16[128,3584]{1,0:T(8,128)(2,1)} %refs_6_.1), channel_id=1, source_target_pairs={{0,8},{1,9},{2,10},{3,11},{4,12},{5,13},{6,14},{7,15},{8,0},{9,1},... | collective-permute-start | bytes 2752520 | tf_op jit(solution)/shard_map/ppermute | solution.py:143
  11.9 13.6 %collective-permute-start.9 = (bf16[256,1024]{1,0:T(8,128)(2,1)}, bf16[256,1024]{1,0:T(8,128)(2,1)}, u32[]{:S(2)}, u32[]{:S(2)}) collective-permute-start(bf16[256,1024]{1,0:T(8,128)(2,1)} %pad_maximum_fusion.5.refs_0_), channel_id=1, source_target_pairs={{0,1},{1,0},{2,3},{3,2},{4,5},{5,4},{6,7},{7,6},{8,9},{9,8},{10,11... | collective-permute-start | bytes 1572872 | tf_op jit(solution)/shard_map/ppermute | solution.py:143
  21.7 14.4 %collective-permute-start.1 = (bf16[136,2048]{1,0:T(8,128)(2,1)S(1)}, bf16[136,2048]{1,0:T(8,128)(2,1)S(1)}, u32[]{:S(2)}, u32[]{:S(2)}) collective-permute-start(bf16[136,2048]{1,0:T(8,128)(2,1)S(1)} %pad_maximum_fusion), channel_id=1, source_target_pairs={{0,1},{3,2},{4,5},{7,6},{8,9},{11,10},{12,13},{15,14},{16,17},{19,... | collective-permute-start | bytes 1671176 | tf_op jit(solution)/shard_map/ppermute | solution.py:143
  24.1 3.6 %collective-permute-start.10 = (bf16[256,1024]{1,0:T(8,128)(2,1)}, bf16[256,1024]{1,0:T(8,128)(2,1)}, u32[]{:S(2)}, u32[]{:S(2)}) collective-permute-start(bf16[256,1024]{1,0:T(8,128)(2,1)} %pad_maximum_fusion.5.refs_0_), channel_id=1, source_target_pairs={{1,2},{2,1},{5,6},{6,5},{9,10},{10,9},{13,14},{14,13},{17,18},{18,... | collective-permute-start | bytes 1572872 | tf_op jit(solution)/shard_map/ppermute | solution.py:143
  25.6 5.0 %collective-permute-start.11 = (bf16[256,1024]{1,0:T(8,128)(2,1)}, bf16[256,1024]{1,0:T(8,128)(2,1)}, u32[]{:S(2)}, u32[]{:S(2)}) collective-permute-start(bf16[256,1024]{1,0:T(8,128)(2,1)} %collective-permute-done.9.refs_1_), channel_id=1, source_target_pairs={{1,2},{2,1},{5,6},{6,5},{9,10},{10,9},{13,14},{14,13},{17,18},{18,... | collective-permute-start | bytes 1572872 | tf_op jit(solution)/shard_map/ppermute | solution.py:143
  27.7 55.1 %collective-permute-start.12 = (bf16[256,1024]{1,0:T(8,128)(2,1)}, bf16[256,1024]{1,0:T(8,128)(2,1)}, u32[]{:S(2)}, u32[]{:S(2)}) collective-permute-start(bf16[256,1024]{1,0:T(8,128)(2,1)} %collective-permute-done.10.refs_2_), channel_id=1, source_target_pairs={{1,0},{2,3},{5,4},{6,7},{9,8},{10,11},{13,12},{14,15},{17,16},{18,... | collective-permute-start | bytes 1572872 | tf_op jit(solution)/shard_map/ppermute | solution.py:143
  30.3 34.5 %collective-permute-start.16 = (bf16[128,3584]{1,0:T(8,128)(2,1)}, bf16[128,3584]{1,0:T(8,128)(2,1)}, u32[]{:S(2)}, u32[]{:S(2)}) collective-permute-start(bf16[128,3584]{1,0:T(8,128)(2,1)} %collective-permute-done.14.refs_7_), channel_id=1, source_target_pairs={{0,8},{1,9},{2,10},{3,11},{4,12},{5,13},{6,14},{7,15},{8,0},{9,1},... | collective-permute-start | bytes 2752520 | tf_op jit(solution)/shard_map/ppermute | solution.py:143
  30.6 53.5 %collective-permute-start.15 = (bf16[128,3584]{1,0:T(8,128)(2,1)}, bf16[128,3584]{1,0:T(8,128)(2,1)}, u32[]{:S(2)}, u32[]{:S(2)}) collective-permute-start(bf16[128,3584]{1,0:T(8,128)(2,1)} %collective-permute-done.14.refs_7_), channel_id=1, source_target_pairs={{0,4},{1,5},{2,6},{3,7},{4,0},{5,1},{6,2},{7,3},{8,12},{9,13},{10,... | collective-permute-start | bytes 2752520 | tf_op jit(solution)/shard_map/ppermute | solution.py:143
  30.6 8.5 %collective-permute-start.3 = (bf16[128,3584]{1,0:T(8,128)(2,1)}, bf16[128,3584]{1,0:T(8,128)(2,1)}, u32[]{:S(2)}, u32[]{:S(2)}) collective-permute-start(bf16[128,3584]{1,0:T(8,128)(2,1)} %collective-permute-done.2.refs_10_), channel_id=1, source_target_pairs={{0,4},{1,5},{2,6},{3,7},{4,0},{5,1},{6,2},{7,3},{8,12},{9,13},{10,... | collective-permute-start | bytes 2752520 | tf_op jit(solution)/shard_map/ppermute | solution.py:143
  36.1 47.9 %collective-permute-start.13 = (bf16[256,1024]{1,0:T(8,128)(2,1)}, bf16[256,1024]{1,0:T(8,128)(2,1)}, u32[]{:S(2)}, u32[]{:S(2)}) collective-permute-start(bf16[256,1024]{1,0:T(8,128)(2,1)} %collective-permute-done.11.refs_3_), channel_id=1, source_target_pairs={{1,0},{2,3},{5,4},{6,7},{9,8},{10,11},{13,12},{14,15},{17,16},{18,... | collective-permute-start | bytes 1572872 | tf_op jit(solution)/shard_map/ppermute | solution.py:143
  39.1 30.2 %collective-permute-start.5 = (bf16[136,2048]{1,0:T(8,128)(2,1)S(1)}, bf16[136,2048]{1,0:T(8,128)(2,1)S(1)}, u32[]{:S(2)}, u32[]{:S(2)}) collective-permute-start(bf16[136,2048]{1,0:T(8,128)(2,1)S(1)} %pad_maximum_fusion.2), channel_id=1, source_target_pairs={{2,1},{3,2},{6,5},{7,6},{8,9},{9,10},{12,13},{13,14},{18,17},{19,1... | collective-permute-start | bytes 1671176 | tf_op jit(solution)/shard_map/ppermute | solution.py:143
  64.8 16.0 %collective-permute-start.4 = (bf16[136,2048]{1,0:T(8,128)(2,1)S(1)}, bf16[136,2048]{1,0:T(8,128)(2,1)S(1)}, u32[]{:S(2)}, u32[]{:S(2)}) collective-permute-start(bf16[136,2048]{1,0:T(8,128)(2,1)S(1)} %pad_maximum_fusion.1), channel_id=1, source_target_pairs={{0,1},{1,0},{2,3},{3,2},{4,5},{5,4},{6,7},{7,6},{8,9},{9,8},{10,11... | collective-permute-start | bytes 1671176 | tf_op jit(solution)/shard_map/ppermute | solution.py:143
  69.3 14.8 %collective-permute-start.17 = (bf16[128,3584]{1,0:T(8,128)(2,1)}, bf16[128,3584]{1,0:T(8,128)(2,1)}, u32[]{:S(2)}, u32[]{:S(2)}) collective-permute-start(bf16[128,3584]{1,0:T(8,128)(2,1)} %collective-permute-done.16.refs_11_), channel_id=1, source_target_pairs={{0,4},{1,5},{2,6},{3,7},{4,0},{5,1},{6,2},{7,3},{8,12},{9,13},{10,... | collective-permute-start | bytes 2752520 | tf_op jit(solution)/shard_map/ppermute | solution.py:143
  80.8 17.3 %collective-permute-start.6 = (bf16[136,2048]{1,0:T(8,128)(2,1)S(1)}, bf16[136,2048]{1,0:T(8,128)(2,1)S(1)}, u32[]{:S(2)}, u32[]{:S(2)}) collective-permute-start(bf16[136,2048]{1,0:T(8,128)(2,1)S(1)} %pad_maximum_fusion.3), channel_id=1, source_target_pairs={{1,0},{2,1},{5,4},{6,5},{9,10},{10,11},{13,14},{14,15},{17,16},{18... | collective-permute-start | bytes 1671176 | tf_op jit(solution)/shard_map/ppermute | solution.py:143
  82.8 28.9 %collective-permute-start.7 = (bf16[136,2048]{1,0:T(8,128)(2,1)S(1)}, bf16[136,2048]{1,0:T(8,128)(2,1)S(1)}, u32[]{:S(2)}, u32[]{:S(2)}) collective-permute-start(bf16[136,2048]{1,0:T(8,128)(2,1)S(1)} %pad_maximum_fusion.4), channel_id=1, source_target_pairs={{0,2},{1,3},{4,6},{5,7},{10,8},{11,9},{14,12},{15,13},{16,18},{17,... | collective-permute-start | bytes 1671176 | tf_op jit(solution)/shard_map/ppermute | solution.py:143
